TPU v7x, 32 devices: a whole 2x2x4 slice. The times are simulated.
32 devices in a mesh: fsdp: 4 (over y, x), ctx: 8 (over z, core).
Axes of the slice: x: 2, y: 2, z: 4, core: 2. Of those that a mesh axis runs over, the one named last changes fastest.
Arguments:
- block_input: bfloat16 [8, 512, 1088], P('fsdp', 'ctx'), may hold values from -6 to 6
- positions: int32 [8, 512], P('fsdp', 'ctx'), may hold values from 0 to 511, as said below
- prefix: int32 [8], P('fsdp'), may hold values from 0 to 255
- first_gain: float32 [1088], replicated, may hold values from 0.25 to 1.75
- first_bias: float32 [1088], replicated, may hold values from -3 to 3
- query_key_value: bfloat16 [1088, 3264], P('fsdp')
- query_value_bias: float32 [2, 1088], replicated, may hold values from -3 to 3
- output_weight: bfloat16 [1088, 1088], P('fsdp'), may hold values from -1.5 to 1.5
- output_bias: float32 [1088], replicated, may hold values from -3 to 3
- second_gain: float32 [1088], replicated, may hold values from 0.25 to 1.75
- second_bias: float32 [1088], replicated, may hold values from -3 to 3
- expand_weight: bfloat16 [1088, 4352], P('fsdp'), may hold values from -0.1875 to 0.1875
- expand_bias: float32 [4352], replicated, may hold values from -3 to 3
- contract_weight: bfloat16 [4352, 1088], P('fsdp'), may hold values from -0.09375 to 0.09375
- contract_bias: float32 [1088], replicated, may hold values from -3 to 3
- cotangent: bfloat16 [8, 512, 1088], P('fsdp', 'ctx'), may hold values from -6 to 6
Outputs:
- block_output: bfloat16 [8, 512, 1088], P('fsdp', 'ctx')
- input_gradient: float32 [8, 512, 1088], P('fsdp', 'ctx')
- first_gain_gradient: float32 [1088], replicated
- first_bias_gradient: float32 [1088], replicated
- query_key_value_gradient: float32 [1088, 3264], P('fsdp')
- query_value_bias_gradient: float32 [2, 1088], replicated
- output_weight_gradient: float32 [1088, 1088], P('fsdp')
- output_bias_gradient: float32 [1088], replicated
- second_gain_gradient: float32 [1088], replicated
- second_bias_gradient: float32 [1088], replicated
- expand_weight_gradient: float32 [1088, 4352], P('fsdp')
- expand_bias_gradient: float32 [4352], replicated
- contract_weight_gradient: float32 [4352, 1088], P('fsdp')
- contract_bias_gradient: float32 [1088], replicated
Inputs may be any that keep to these rules, and one draw needn't show every extreme that they name: Each row lists the positions 0 to 511 once, as blocks of 64 consecutive increasing positions whose order along the row is arbitrary; a device's tokens of a sequence form one such block.
All inputs are finite; a program needn't handle non-finite values.
Results may differ from a plain program's by a relative error of at most 0.017.
Values may be sent and summed in bfloat16 or wider, within the bound.
No kernel may reach another device: no remote copies, remote signals or barrier semaphores. Data moves between devices by JAX's collectives and lax.ppermute only.
A program may use at most 256 MiB of HBM per device.

v0:
```python
import jax
import jax.numpy as jnp
from jax import lax
from jax.sharding import PartitionSpec as P

HEAD_DIM = 64
EPSILON = 1e-05
NEGATIVE = -1e30


def layer_norm(values, gain, bias):
    center = values - jnp.mean(values, axis=-1, keepdims=True)
    inverse = lax.rsqrt(jnp.mean(center * center, axis=-1, keepdims=True) + EPSILON)
    normed = center * inverse
    return (normed * gain + bias, normed, inverse)


def norm_back(upper, normed, inverse, gain):
    scaled = upper * gain
    return inverse * (
        scaled
        - jnp.mean(scaled, axis=-1, keepdims=True)
        - normed * jnp.mean(scaled * normed, axis=-1, keepdims=True)
    )


def gelu(values):
    return jax.nn.gelu(values, approximate=True)


def term_of(left, right):
    return jnp.einsum("ti,tj->ij", left, right, preferred_element_type=jnp.float32)


def per_device(
    block_input,
    positions,
    prefix,
    first_gain,
    first_bias,
    query_key_value,
    query_value_bias,
    output_weight,
    output_bias,
    second_gain,
    second_bias,
    expand_weight,
    expand_bias,
    contract_weight,
    contract_bias,
    cotangent,
):
    sequences, piece, width = block_input.shape
    heads = width // HEAD_DIM
    scale = HEAD_DIM ** (-0.5)
    rows = sequences * piece
    joint_full, output_full, expand_full, contract_full = (
        lax.all_gather(query_key_value, "fsdp", axis=0, tiled=True),
        lax.all_gather(output_weight, "fsdp", axis=0, tiled=True),
        lax.all_gather(expand_weight, "fsdp", axis=0, tiled=True),
        lax.all_gather(contract_weight, "fsdp", axis=0, tiled=True),
    )
    all_places = lax.all_gather(positions, "ctx", axis=1, tiled=True)
    limits = jnp.maximum(positions, prefix[:, None] - 1)
    input_rows = block_input.reshape(rows, width).astype(jnp.float32)
    first_out, first_normed, first_inverse = layer_norm(input_rows, first_gain, first_bias)
    first_round = first_out.astype(jnp.bfloat16)
    joint = jnp.dot(first_round, joint_full, preferred_element_type=jnp.float32)
    query = (joint[:, :width] + query_value_bias[0]).astype(jnp.bfloat16)
    keys = joint[:, width : 2 * width].astype(jnp.bfloat16)
    values = (joint[:, 2 * width :] + query_value_bias[1]).astype(jnp.bfloat16)
    query_heads = query.reshape(sequences, piece, heads, HEAD_DIM)
    key_rows = keys.reshape(sequences, piece, width)
    value_rows = values.reshape(sequences, piece, width)
    key_piece = lax.all_gather(key_rows, "ctx", axis=1, tiled=True)
    top = jnp.full((sequences, heads, piece), NEGATIVE, jnp.float32)
    count = key_piece.shape[1]
    fold_key_heads = key_piece.reshape(sequences, count, heads, HEAD_DIM)
    scores = (
        jnp.einsum(
            "bqhd,bkhd->bhqk", query_heads, fold_key_heads, preferred_element_type=jnp.float32
        )
        * scale
    )
    visible = all_places[:, None, None, :] <= limits[:, None, :, None]
    new_top = jnp.maximum(top, jnp.max(jnp.where(visible, scores, NEGATIVE), axis=-1))
    weights = jnp.where(visible, jnp.exp(scores - new_top[..., None]), 0.0)
    total = jnp.sum(weights, axis=-1)
    top, total = (new_top, total)
    log_heads = top + jnp.log(total)

    def fold_keys(pieces):
        key_piece, value_piece = pieces
        count = key_piece.shape[1]
        key_heads = key_piece.reshape(sequences, count, heads, HEAD_DIM)
        value_heads = value_piece.reshape(sequences, count, heads, HEAD_DIM)
        scores = (
            jnp.einsum(
                "bqhd,bkhd->bhqk", query_heads, key_heads, preferred_element_type=jnp.float32
            )
            * scale
        )
        visible = all_places[:, None, None, :] <= limits[:, None, :, None]
        shares = jnp.where(visible, jnp.exp(scores - log_heads[..., None]), 0.0).astype(
            jnp.bfloat16
        )
        return jnp.einsum(
            "bhqk,bkhd->bqhd", shares, value_heads, preferred_element_type=jnp.float32
        )

    summed = fold_keys(
        (
            lax.all_gather(key_rows, "ctx", axis=1, tiled=True),
            lax.all_gather(value_rows, "ctx", axis=1, tiled=True),
        )
    )
    mixed = summed.astype(jnp.bfloat16).reshape(rows, width)
    log_total = jnp.swapaxes(log_heads, 1, 2)
    residual = (
        input_rows + jnp.dot(mixed, output_full, preferred_element_type=jnp.float32) + output_bias
    )
    second_out, second_normed, second_inverse = layer_norm(residual, second_gain, second_bias)
    second_round = second_out.astype(jnp.bfloat16)
    before = jnp.dot(second_round, expand_full, preferred_element_type=jnp.float32) + expand_bias
    after, gelu_back = jax.vjp(gelu, before)
    after_round = after.astype(jnp.bfloat16)
    block_output = (
        (
            residual
            + jnp.dot(after_round, contract_full, preferred_element_type=jnp.float32)
            + contract_bias
        )
        .astype(jnp.bfloat16)
        .reshape(sequences, piece, width)
    )
    joint_full, output_full, expand_full, contract_full = (
        lax.all_gather(query_key_value, "fsdp", axis=0, tiled=True),
        lax.all_gather(output_weight, "fsdp", axis=0, tiled=True),
        lax.all_gather(expand_weight, "fsdp", axis=0, tiled=True),
        lax.all_gather(contract_weight, "fsdp", axis=0, tiled=True),
    )
    upper = cotangent.reshape(rows, width)
    upper_wide = upper.astype(jnp.float32)
    after_grad = jnp.dot(upper, contract_full.T, preferred_element_type=jnp.float32)
    before_grad = gelu_back(after_grad)[0]
    before_round = before_grad.astype(jnp.bfloat16)
    second_grad = jnp.dot(before_round, expand_full.T, preferred_element_type=jnp.float32)
    residual_grad = upper_wide + norm_back(second_grad, second_normed, second_inverse, second_gain)
    residual_round = residual_grad.astype(jnp.bfloat16)
    mixed_grad = jnp.dot(residual_round, output_full.T, preferred_element_type=jnp.float32).astype(
        jnp.bfloat16
    )
    flows = jnp.sum(
        (mixed_grad.astype(jnp.float32) * mixed.astype(jnp.float32)).reshape(
            sequences, piece, heads, HEAD_DIM
        ),
        axis=-1,
    )
    all_query, all_upper = (
        lax.all_gather(query.reshape(sequences, piece, width), "ctx", axis=1, tiled=True),
        lax.all_gather(mixed_grad.reshape(sequences, piece, width), "ctx", axis=1, tiled=True),
    )
    all_log, all_flows = (
        lax.all_gather(log_total, "ctx", axis=1, tiled=True),
        lax.all_gather(flows, "ctx", axis=1, tiled=True),
    )
    all_limits = jnp.maximum(all_places, prefix[:, None] - 1)
    length = all_query.shape[1]
    span = min(512, length)
    key_heads = keys.reshape(sequences, piece, heads, HEAD_DIM)
    value_heads = values.reshape(sequences, piece, heads, HEAD_DIM)

    def back_block(number, state):
        key_grad, value_grad, terms = state
        start = number * span
        part = lax.dynamic_slice_in_dim(all_query, start, span, 1).reshape(
            sequences, span, heads, HEAD_DIM
        )
        above = lax.dynamic_slice_in_dim(all_upper, start, span, 1).reshape(
            sequences, span, heads, HEAD_DIM
        )
        log_part = lax.dynamic_slice_in_dim(all_log, start, span, 1)
        flow_part = lax.dynamic_slice_in_dim(all_flows, start, span, 1)
        limit = lax.dynamic_slice_in_dim(all_limits, start, span, 1)
        scores = (
            jnp.einsum("bqhd,bkhd->bhqk", part, key_heads, preferred_element_type=jnp.float32)
            * scale
        )
        visible = positions[:, None, None, :] <= limit[:, None, :, None]
        shares = jnp.where(visible, jnp.exp(scores - jnp.swapaxes(log_part, 1, 2)[..., None]), 0.0)
        share_grad = jnp.einsum(
            "bqhd,bkhd->bhqk", above, value_heads, preferred_element_type=jnp.float32
        )
        score_grad = shares * (share_grad - jnp.swapaxes(flow_part, 1, 2)[..., None])
        score_round = score_grad.astype(jnp.bfloat16)
        key_grad = (
            key_grad
            + jnp.einsum("bhqk,bqhd->bkhd", score_round, part, preferred_element_type=jnp.float32)
            * scale
        )
        value_grad = value_grad + jnp.einsum(
            "bhqk,bqhd->bkhd",
            shares.astype(jnp.bfloat16),
            above,
            preferred_element_type=jnp.float32,
        )
        query_grad = (
            jnp.einsum(
                "bhqk,bkhd->bqhd", score_round, key_heads, preferred_element_type=jnp.float32
            )
            * scale
        )
        terms = lax.dynamic_update_slice_in_dim(
            terms, query_grad.reshape(sequences, span, width), start, 1
        )
        return (key_grad, value_grad, terms)

    zero_heads = jnp.zeros((sequences, piece, heads, HEAD_DIM), jnp.float32)
    empty_terms = jnp.zeros((sequences, length, width), jnp.float32)
    key_grad, value_grad, terms = lax.fori_loop(
        0, length // span, back_block, (zero_heads, zero_heads, empty_terms)
    )
    query_grad = lax.psum_scatter(terms, "ctx", scatter_dimension=1, tiled=True).reshape(
        rows, width
    )
    key_grad = key_grad.reshape(rows, width)
    value_grad = value_grad.reshape(rows, width)
    joint_grad = jnp.concatenate([query_grad, key_grad, value_grad], axis=1).astype(jnp.bfloat16)
    first_grad = jnp.dot(joint_grad, joint_full.T, preferred_element_type=jnp.float32)
    input_gradient = (
        residual_grad + norm_back(first_grad, first_normed, first_inverse, first_gain)
    ).reshape(sequences, piece, width)
    joint_share = lax.psum_scatter(
        term_of(first_round, joint_grad), "fsdp", scatter_dimension=0, tiled=True
    )
    output_share = lax.psum_scatter(
        term_of(mixed, residual_round), "fsdp", scatter_dimension=0, tiled=True
    )
    expand_share = lax.psum_scatter(
        term_of(second_round, before_round), "fsdp", scatter_dimension=0, tiled=True
    )
    contract_share = lax.psum_scatter(
        term_of(after_round, upper), "fsdp", scatter_dimension=0, tiled=True
    )
    joint_sum, output_sum, expand_sum, contract_sum = lax.psum(
        (joint_share, output_share, expand_share, contract_share), "ctx"
    )
    small = lax.psum(
        (
            jnp.sum(first_grad * first_normed, axis=0),
            jnp.sum(first_grad, axis=0),
            jnp.stack([jnp.sum(query_grad, axis=0), jnp.sum(value_grad, axis=0)]),
            jnp.sum(residual_grad, axis=0),
            jnp.sum(second_grad * second_normed, axis=0),
            jnp.sum(second_grad, axis=0),
            jnp.sum(before_grad, axis=0),
            jnp.sum(upper_wide, axis=0),
        ),
        ("fsdp", "ctx"),
    )
    return (
        block_output,
        input_gradient,
        small[0],
        small[1],
        joint_sum,
        small[2],
        output_sum,
        small[3],
        small[4],
        small[5],
        expand_sum,
        small[6],
        contract_sum,
        small[7],
    )


def solution(mesh):
    in_specs = (
        P("fsdp", "ctx", None),
        P("fsdp", "ctx"),
        P("fsdp"),
        P(),
        P(),
        P("fsdp", None),
        P(),
        P("fsdp", None),
        P(),
        P(),
        P(),
        P("fsdp", None),
        P(),
        P("fsdp", None),
        P(),
        P("fsdp", "ctx", None),
    )
    out_specs = (
        P("fsdp", "ctx", None),
        P("fsdp", "ctx", None),
        P(),
        P(),
        P("fsdp", None),
        P(),
        P("fsdp", None),
        P(),
        P(),
        P(),
        P("fsdp", None),
        P(),
        P("fsdp", None),
        P(),
    )
    return jax.shard_map(
        per_device, mesh=mesh, in_specs=in_specs, out_specs=out_specs, check_vma=False
    )
```

profile of v0, /device:TPU:0, one launch (start us, length us, event | category | flops | bytes accessed | tf_op | source)
XLA Modules:
  0.0 1415.7 jit_solution(14344551594454998313)
XLA Ops:
  9.5 81.1 %all-gather.10.cloned.1.call-done = bf16[1088,3264]{1,0:T(8,128)(2,1)} async-done(((bf16[272,3264]{1,0:T(8,128)(2,1)}), bf16[1088,3264]{1,0:T(8,128)(2,1)}) %all-gather.10.cloned.1.call-update) | async-done | bytes 7102480 | tf_op jit(solution)/shard_map/all_gather | solution.py:58
  90.5 6.3 fusion.48
  100.5 11.7 all-gather
  114.6 78.9 %all-gather.20.cloned.1.call-done = bf16[4352,1088]{1,0:T(8,128)(2,1)} async-done(((bf16[1088,1088]{1,0:T(8,128)(2,1)}), bf16[4352,1088]{1,0:T(8,128)(2,1)}) %all-gather.20.cloned.1.call-update) | async-done | bytes 9469968 | tf_op jit(solution)/shard_map/all_gather | solution.py:61
  193.5 8.0 fusion.56
  201.5 25.7 %all-gather.14.cloned.1.call-done = bf16[2,512,1088]{2,1,0:T(8,128)(2,1)} async-done(((bf16[2,64,1088]{2,1,0:T(8,128)(2,1)}), bf16[2,512,1088]{2,1,0:T(8,128)(2,1)}) %all-gather.14.cloned.1.call-update) | async-done | bytes 2228240 | tf_op jit(solution)/shard_map/all_gather | solution.py:113
  233.2 26.7 %all-gather.12.cloned.1.call-done = bf16[2,512,1088]{2,1,0:T(8,128)(2,1)} async-done(((bf16[2,64,1088]{2,1,0:T(8,128)(2,1)}), bf16[2,512,1088]{2,1,0:T(8,128)(2,1)}) %all-gather.12.cloned.1.call-update) | async-done | bytes 2228240 | tf_op jit(solution)/shard_map/all_gather | solution.py:114
  267.5 31.9 %all-gather.16.cloned.1.call-done = bf16[1088,1088]{1,0:T(8,128)(2,1)} async-done(((bf16[272,1088]{1,0:T(8,128)(2,1)}), bf16[1088,1088]{1,0:T(8,128)(2,1)}) %all-gather.16.cloned.1.call-update) | async-done | bytes 2367504 | tf_op jit(solution)/shard_map/all_gather | solution.py:59
  302.5 95.1 %all-gather.18.cloned.1.call-done = bf16[1088,4352]{1,0:T(8,128)(2,1)} async-done(((bf16[272,4352]{1,0:T(8,128)(2,1)}), bf16[1088,4352]{1,0:T(8,128)(2,1)}) %all-gather.18.cloned.1.call-update) | async-done | bytes 9469968 | tf_op jit(solution)/shard_map/all_gather | solution.py:60
  397.7 9.7 fusion.50
  417.8 17.2 %all_gather.48 = f32[2,512,17]{2,0,1:T(2,128)S(1)} all-gather(f32[2,64,17]{2,0,1:T(2,128)S(1)} %copy.114), channel_id=1, replica_groups=mesh['fsdp'=4,'ctx'=8] {'ctx'}, dimensions={1}, use_global_device_ids=true | all-gather | bytes 78336 | tf_op jit(solution)/shard_map/all_gather | solution.py:165
  435.4 16.0 %all_gather.46 = f32[2,512,17]{2,0,1:T(2,128)S(1)} all-gather(f32[2,64,17]{2,0,1:T(2,128)S(1)} %copy.109), channel_id=1, replica_groups=mesh['fsdp'=4,'ctx'=8] {'ctx'}, dimensions={1}, use_global_device_ids=true | all-gather | bytes 78336 | tf_op jit(solution)/shard_map/all_gather | solution.py:164
  458.5 10.4 all-gather.24.cloned.1.call-done
  491.5 9.6 fusion.33
  501.1 11.4 fusion.49
  524.8 15.9 %reduce-scatter.8.cloned.1.call-done = f32[2,64,1088]{2,1,0:T(8,128)} async-done(((f32[2,512,1088]{2,1,0:T(8,128)}), f32[2,64,1088]{2,1,0:T(8,128)}) %reduce-scatter.8.cloned.1.call-update) | async-done | bytes 557072 | tf_op jit(solution)/shard_map/reduce_scatter | solution.py:223
  542.5 7.8 fusion.47
  550.4 51.7 %reduce-scatter.16.cloned.1.call-done = f32[272,1088]{1,0:T(8,128)} async-done(((f32[1088,1088]{1,0:T(8,128)}), f32[272,1088]{1,0:T(8,128)}) %reduce-scatter.16.cloned.1.call-update) | async-done | bytes 1183760
  602.1 175.7 %reduce-scatter.12.cloned.1.call-done = f32[272,4352]{1,0:T(8,128)} async-done(((f32[1088,4352]{1,0:T(8,128)}), f32[272,4352]{1,0:T(8,128)}) %reduce-scatter.12.cloned.1.call-update) | async-done | bytes 4734992 | tf_op jit(solution)/shard_map/reduce_scatter | solution.py:239
  777.8 183.3 %reduce-scatter.14.cloned.1.call-done = f32[1088,1088]{1,0:T(8,128)} async-done(((f32[4352,1088]{1,0:T(8,128)}), f32[1088,1088]{1,0:T(8,128)}) %reduce-scatter.14.cloned.1.call-update) | async-done | bytes 4734992 | tf_op jit(solution)/shard_map/reduce_scatter | solution.py:242
  961.1 139.3 %reduce-scatter.10.cloned.1.call-done = f32[272,3264]{1,0:T(8,128)} async-done(((f32[1088,3264]{1,0:T(8,128)}), f32[272,3264]{1,0:T(8,128)}) %reduce-scatter.10.cloned.1.call-update) | async-done | bytes 3551248 | tf_op jit(solution)/shard_map/reduce_scatter | solution.py:233
  1101.5 8.1 fusion.3
  1117.3 43.6 %all-reduce.1 = (f32[1088]{0:T(1024)}, f32[1088]{0:T(1024)}, f32[2,1088]{1,0:T(2,128)}, f32[1088]{0:T(1024)}, f32[1088]{0:T(1024)}, /*index=5*/f32[1088]{0:T(1024)}, f32[4352]{0:T(1024)}, f32[1088]{0:T(1024)}) all-reduce(f32[1088]{0:T(1024)S(1)} %get-tuple-element.69, ...), channel_id=1, replica_groups=mesh['fsdp'=4,'ctx'=8] {'fsdp','ctx'}, use_global_device_ids=true, to_apply=%region_13.14 | all-reduce | flops 13056 | bytes 104448 | tf_op jit(solution)/shard_map/psum | solution.py:248
  1160.9 237.0 %all-reduce.5.cloned.1.call-done = (f32[272,3264]{1,0:T(8,128)}, f32[272,1088]{1,0:T(8,128)}, f32[272,4352]{1,0:T(8,128)}, f32[1088,1088]{1,0:T(8,128)}) async-done(((f32[272,3264]{1,0:T(8,128)}, f32[272,1088]{1,0:T(8,128)}, f32[272,4352]{1,0:T(8,128)}, f32[1088,1088]{1,0:T(8,128)}), (f32[272,3264]{1,0:T(8,128)}, f32[272,1088]{1,0:T(8,128)}, f32[272,4352]{1,0:T(8,128)}, ...) | async-done | bytes 14204944 | tf_op jit(solution)/shard_map/psum | solution.py:245
  (203 shorter events, 98.7 us)
Async XLA Ops:
  7.2 83.3 %all-gather.10.cloned.1.call-start = ((), (), s32[]{:S(2)}) async-start(), calls=%async_computation.5 | async-start | bytes 9052160 | tf_op jit(solution)/shard_map/all_gather | solution.py:58
  7.9 82.6 %copy-start.23 = (f32[1088]{0:T(1024)S(1)}, f32[1088]{0:T(1024)}, u32[]{:S(2)}) copy-start(f32[1088]{0:T(1024)} %param.19) | copy-start | bytes 13060
  7.9 82.6 %copy-start.26 = (f32[1088]{0:T(1024)S(1)}, f32[1088]{0:T(1024)}, u32[]{:S(2)}) copy-start(f32[1088]{0:T(1024)} %param.20) | copy-start | bytes 13060
  7.9 185.6 %all-gather.20.cloned.1.call-start = ((), (), s32[]{:S(2)}) async-start(), calls=%async_computation.10 | async-start | bytes 12533760 | tf_op jit(solution)/shard_map/all_gather | solution.py:61
  8.7 218.5 %all-gather.14.cloned.1.call-start = ((), (), s32[]{:S(2)}) async-start(), calls=%async_computation.7 | async-start | bytes 2654208 | tf_op jit(solution)/shard_map/all_gather | solution.py:113
  9.1 81.4 %copy-start.34 = (f32[128]{0:T(128)}, f32[128]{0:T(128)S(1)}, u32[]{:S(2)}) copy-start(f32[128]{0:T(128)S(1)} %div.27) | copy-start | bytes 1540
  9.5 88.4 %copy-start.41 = (f32[2,1088]{1,0:T(2,128)S(1)}, f32[2,1088]{1,0:T(2,128)}, u32[]{:S(2)}) copy-start(f32[2,1088]{1,0:T(2,128)} %param.22) | copy-start | bytes 26116
  97.8 162.1 %all-gather.12.cloned.1.call-start = ((), (), s32[]{:S(2)}) async-start(), calls=%async_computation.6 | async-start | bytes 2654208 | tf_op jit(solution)/shard_map/all_gather | solution.py:114
  99.3 200.2 %all-gather.16.cloned.1.call-start = ((), (), s32[]{:S(2)}) async-start(), calls=%async_computation.8 | async-start | bytes 3133440 | tf_op jit(solution)/shard_map/all_gather | solution.py:59
  99.9 297.8 %all-gather.18.cloned.1.call-start = ((), (), s32[]{:S(2)}) async-start(), calls=%async_computation.9 | async-start | bytes 11837440 | tf_op jit(solution)/shard_map/all_gather | solution.py:60
  100.4 351.1 %all-gather.22.cloned.1.call-start = ((), (), s32[]{:S(2)}) async-start(), calls=%async_computation.11 | async-start | bytes 2654208 | tf_op jit(solution)/shard_map/all_gather | solution.py:160
  114.6 354.3 %all-gather.24.cloned.1.call-start = ((), (), s32[]{:S(2)}) async-start(), calls=%async_computation.12 | async-start | bytes 2654208 | tf_op jit(solution)/shard_map/all_gather | solution.py:161
  267.5 144.3 %copy-start.8 = (bf16[128,1088]{0,1:T(8,128)(2,1)}, bf16[128,1088]{0,1:T(8,128)(2,1)S(1)}, u32[]{:S(2)}) copy-start(bf16[128,1088]{0,1:T(8,128)(2,1)S(1)} %reshape.201) | copy-start | bytes 835588
  267.5 130.2 %copy-start.22 = (f32[1088]{0:T(1024)S(1)}, f32[1088]{0:T(1024)}, u32[]{:S(2)}) copy-start(f32[1088]{0:T(1024)} %param.25) | copy-start | bytes 13060
  267.5 130.2 %copy-start.24 = (f32[1088]{0:T(1024)S(1)}, f32[1088]{0:T(1024)}, u32[]{:S(2)}) copy-start(f32[1088]{0:T(1024)} %param.26) | copy-start | bytes 13060
  267.5 130.2 %copy-start.43 = (f32[4352]{0:T(1024)S(1)}, f32[4352]{0:T(1024)}, u32[]{:S(2)}) copy-start(f32[4352]{0:T(1024)} %param.28) | copy-start | bytes 52228
  302.3 108.4 %copy-start.32 = (f32[128]{0:T(128)}, f32[128]{0:T(128)S(1)}, u32[]{:S(2)}) copy-start(f32[128]{0:T(128)S(1)} %broadcast_multiply_fusion.6) | copy-start | bytes 1540
  302.5 108.2 %copy-start.38 = (f32[128]{0:T(128)}, f32[128]{0:T(128)S(1)}, u32[]{:S(2)}) copy-start(f32[128]{0:T(128)S(1)} %add_rsqrt_fusion.1) | copy-start | bytes 1540
  413.6 127.1 %reduce-scatter.8.cloned.1.call-start = ((), (), s32[]{:S(2)}) async-start(), calls=%async_computation.13 | async-start | bytes 5308416 | tf_op jit(solution)/shard_map/reduce_scatter | solution.py:223
  486.5 115.6 %reduce-scatter.16.cloned.1.call-start = ((), (), s32[]{:S(2)}) async-start(), calls=%async_computation.17 | async-start | bytes 6266880
  490.8 287.0 %reduce-scatter.12.cloned.1.call-start = ((), (), s32[]{:S(2)}) async-start(), calls=%async_computation.15 | async-start | bytes 23674880 | tf_op jit(solution)/shard_map/reduce_scatter | solution.py:239
  501.1 460.0 %reduce-scatter.14.cloned.1.call-start = ((), (), s32[]{:S(2)}) async-start(), calls=%async_computation.16 | async-start | bytes 25067520 | tf_op jit(solution)/shard_map/reduce_scatter | solution.py:242
  512.5 587.9 %reduce-scatter.10.cloned.1.call-start = ((), (), s32[]{:S(2)}) async-start(), calls=%async_computation.14 | async-start | bytes 18104320 | tf_op jit(solution)/shard_map/reduce_scatter | solution.py:233
  550.3 847.5 %all-reduce.5.cloned.1.call-start = ((), (), s32[]{:S(2)}) async-start(), calls=%async_computation.18 | async-start | bytes 29245440 | tf_op jit(solution)/shard_map/psum | solution.py:245
  (38 other events, 318.5 us)
Sparse Core Ops, SparseCore 0:
  9.8 80.6 all-gather.9
  92.4 101.0 all-gather.19
  195.7 31.4 all-gather.13
  229.2 30.6 all-gather.11
  261.6 37.8 all-gather.15
  301.2 96.4 all-gather.17
  399.3 35.1 all-gather.21
  436.6 32.2 all-gather.23
  486.6 54.0 reduce-scatter.7
  544.2 57.8 reduce-scatter.15
  605.2 172.5 reduce-scatter.11
  780.8 180.2 reduce-scatter.13
  964.3 136.1 reduce-scatter.9
  1103.0 294.8 all-reduce.4
where the time goes:
time: 1420 us
  waiting for transfers between devices  1160 us (82%)
  matrix products  99.5 us (7%)
  blocking collectives  88.6 us (6%)
  local copies, waits for them, and re-layouts  50.5 us (4%)
  between operations  14.8 us (1%)
    psum x1, waiting for transfers between devices, per_device(): lax.psum((joint_share, output_share, expand_share, contract_share), 'ctx')  237 us
    reduce_scatter x1, waiting for transfers between devices, per_device(): lax.psum_scatter(term_of(after_round, upper), 'fsdp', scatter_dimension=0...  183 us
    reduce_scatter x1, waiting for transfers between devices, per_device(): lax.psum_scatter(term_of(second_round, before_round), 'fsdp', scatter_dim...  176 us
    reduce_scatter x1, waiting for transfers between devices, per_device(): lax.psum_scatter(term_of(first_round, joint_grad), 'fsdp', scatter_dimens...  139 us
    all_gather x1, waiting for transfers between devices, per_device(): lax.all_gather(expand_weight, 'fsdp', axis=0, tiled=True)  95.1 us
    all_gather x1, waiting for transfers between devices, per_device(): lax.all_gather(query_key_value, 'fsdp', axis=0, tiled=True)  81.1 us
    all_gather x1, waiting for transfers between devices, per_device(): lax.all_gather(contract_weight, 'fsdp', axis=0, tiled=True)  78.9 us
    unnamed x15, waiting for transfers between devices  54.3 us
  transfers between devices with their start and end apart: 14, of which 13 were waited for; matrix products, arithmetic and copies ran while one was open for 9% of the time, Pallas kernels for 0%

commit v1 on v0

--- a/solution.py
+++ b/solution.py
@@ -6,6 +6,16 @@
 HEAD_DIM = 64
 EPSILON = 1e-05
 NEGATIVE = -1e30
+
+
+def gather_around(x, axis, dim):
+    ways, here, hop = (lax.axis_size(axis), lax.axis_index(axis), x.shape[dim])
+    shape = [n * ways if d == dim else n for d, n in enumerate(x.shape)]
+    full = lax.dynamic_update_slice_in_dim(jnp.zeros(shape, x.dtype), x, here * hop, axis=dim)
+    for far in range(1, ways):
+        x = lax.ppermute(x, axis, [(d, (d + 1) % ways) for d in range(ways)])
+        full = lax.dynamic_update_slice_in_dim(full, x, (here - far) % ways * hop, axis=dim)
+    return full
 
 
 def layer_norm(values, gain, bias):
@@ -55,7 +65,7 @@
     scale = HEAD_DIM ** (-0.5)
     rows = sequences * piece
     joint_full, output_full, expand_full, contract_full = (
-        lax.all_gather(query_key_value, "fsdp", axis=0, tiled=True),
+        gather_around(query_key_value, "fsdp", 0),
         lax.all_gather(output_weight, "fsdp", axis=0, tiled=True),
         lax.all_gather(expand_weight, "fsdp", axis=0, tiled=True),
         lax.all_gather(contract_weight, "fsdp", axis=0, tiled=True),

time: 1420 us -> 1550 us (1.092)
  waiting for transfers between devices: 1160 us -> 1270 us
    ppermute x0 -> x3, waiting for transfers between devices: none -> 115 us  [gather_around(): x = lax.ppermute(x, axis, [(d, (d + 1) % ways) for d in range(ways)])]
    all_gather x1, waiting for transfers between devices: 78.9 us -> 99.7 us  [per_device(): lax.all_gather(contract_weight, 'fsdp', axis=0, tiled=True)]
  transfers between devices with their start and end apart: 14 -> 17, of which waited for: 13 -> 16; matrix products, arithmetic and copies ran while one was open for 9% -> 8% of each run, Pallas kernels for 0% -> 0%
where the time goes in v1:
time: 1550 us
  waiting for transfers between devices  1270 us (82%)
  matrix products  97.2 us (6%)
  blocking collectives  90.5 us (6%)
  local copies, waits for them, and re-layouts  59.5 us (4%)
    psum x1, waiting for transfers between devices, per_device(): lax.psum((joint_share, output_share, expand_share, contract_share), 'ctx')  248 us
    reduce_scatter x1, waiting for transfers between devices, per_device(): lax.psum_scatter(term_of(after_round, upper), 'fsdp', scatter_dimension=0...  183 us
    reduce_scatter x1, waiting for transfers between devices, per_device(): lax.psum_scatter(term_of(second_round, before_round), 'fsdp', scatter_dim...  176 us
    reduce_scatter x1, waiting for transfers between devices, per_device(): lax.psum_scatter(term_of(first_round, joint_grad), 'fsdp', scatter_dimens...  139 us
    ppermute x3, waiting for transfers between devices, gather_around(): x = lax.ppermute(x, axis, [(d, (d + 1) % ways) for d in range(ways)])  115 us
    all_gather x1, waiting for transfers between devices, per_device(): lax.all_gather(contract_weight, 'fsdp', axis=0, tiled=True)  99.7 us
    all_gather x1, waiting for transfers between devices, per_device(): lax.all_gather(expand_weight, 'fsdp', axis=0, tiled=True)  90.2 us
    all_gather x1, waiting for transfers between devices, per_device(): lax.all_gather(query_key_value, 'fsdp', axis=0, tiled=True)  69.7 us
  transfers between devices with their start and end apart: 17, of which 16 were waited for; matrix products, arithmetic and copies ran while one was open for 8% of the time, Pallas kernels for 0%

profile of v1, /device:TPU:0, one launch (start us, length us, event | category | flops | bytes accessed | tf_op | source)
XLA Modules:
  0.0 1546.2 jit_solution(11512471459081106612)
XLA Ops:
  10.2 40.7 %collective-permute-done = bf16[272,3264]{1,0:T(8,128)(2,1)S(1)} collective-permute-done((bf16[272,3264]{1,0:T(8,128)(2,1)}, bf16[272,3264]{1,0:T(8,128)(2,1)S(1)}, u32[]{:S(2)}, u32[]{:S(2)}) %collective-permute-start) | collective-permute-done | bytes 1775648 | tf_op jit(solution)/shard_map/ppermute | solution.py:16
  52.8 39.8 %collective-permute-done.1 = bf16[272,3264]{1,0:T(8,128)(2,1)} collective-permute-done((bf16[272,3264]{1,0:T(8,128)(2,1)S(1)}, bf16[272,3264]{1,0:T(8,128)(2,1)}, u32[]{:S(2)}, u32[]{:S(2)}) %collective-permute-start.1) | collective-permute-done | bytes 1775648 | tf_op jit(solution)/shard_map/ppermute | solution.py:16
  98.7 34.9 %collective-permute-done.2 = bf16[272,3264]{1,0:T(8,128)(2,1)} collective-permute-done((bf16[272,3264]{1,0:T(8,128)(2,1)}, bf16[272,3264]{1,0:T(8,128)(2,1)}, u32[]{:S(2)}, u32[]{:S(2)}) %collective-permute-start.2) | collective-permute-done | bytes 1775648 | tf_op jit(solution)/shard_map/ppermute | solution.py:16
  142.9 11.8 all-gather
  157.1 14.0 all-gather.12.cloned.1.call-done
  177.2 26.8 %all-gather.10.cloned.1.call-done = bf16[2,512,1088]{2,1,0:T(8,128)(2,1)} async-done(((bf16[2,64,1088]{2,1,0:T(8,128)(2,1)}), bf16[2,512,1088]{2,1,0:T(8,128)(2,1)}) %all-gather.10.cloned.1.call-update) | async-done | bytes 2228240 | tf_op jit(solution)/shard_map/all_gather | solution.py:124
  211.3 32.4 %all-gather.14.cloned.1.call-done = bf16[1088,1088]{1,0:T(8,128)(2,1)} async-done(((bf16[272,1088]{1,0:T(8,128)(2,1)}), bf16[1088,1088]{1,0:T(8,128)(2,1)}) %all-gather.14.cloned.1.call-update) | async-done | bytes 2367504 | tf_op jit(solution)/shard_map/all_gather | solution.py:69
  246.8 99.7 %all-gather.18.cloned.1.call-done = bf16[4352,1088]{1,0:T(8,128)(2,1)} async-done(((bf16[1088,1088]{1,0:T(8,128)(2,1)}), bf16[4352,1088]{1,0:T(8,128)(2,1)}) %all-gather.18.cloned.1.call-update) | async-done | bytes 9469968 | tf_op jit(solution)/shard_map/all_gather | solution.py:71
  346.5 8.0 fusion.56
  354.5 90.2 %all-gather.16.cloned.1.call-done = bf16[1088,4352]{1,0:T(8,128)(2,1)} async-done(((bf16[272,4352]{1,0:T(8,128)(2,1)}), bf16[1088,4352]{1,0:T(8,128)(2,1)}) %all-gather.16.cloned.1.call-update) | async-done | bytes 9469968 | tf_op jit(solution)/shard_map/all_gather | solution.py:70
  444.7 9.7 fusion.50
  464.8 17.3 %all_gather.44 = f32[2,512,17]{2,0,1:T(2,128)S(1)} all-gather(f32[2,64,17]{2,0,1:T(2,128)S(1)} %copy.109), channel_id=1, replica_groups=mesh['fsdp'=4,'ctx'=8] {'ctx'}, dimensions={1}, use_global_device_ids=true | all-gather | bytes 78336 | tf_op jit(solution)/shard_map/all_gather | solution.py:174
  493.7 18.3 %all_gather.46 = f32[2,512,17]{2,0,1:T(2,128)} all-gather(f32[2,64,17]{2,0,1:T(2,128)S(1)} %copy.114), channel_id=1, replica_groups=mesh['fsdp'=4,'ctx'=8] {'ctx'}, dimensions={1}, use_global_device_ids=true | all-gather | bytes 78336 | tf_op jit(solution)/shard_map/all_gather | solution.py:175
  542.1 9.6 fusion.33
  552.2 11.4 fusion.49
  575.7 15.8 %reduce-scatter.8.cloned.1.call-done = f32[2,64,1088]{2,1,0:T(8,128)} async-done(((f32[2,512,1088]{2,1,0:T(8,128)}), f32[2,64,1088]{2,1,0:T(8,128)}) %reduce-scatter.8.cloned.1.call-update) | async-done | bytes 557072 | tf_op jit(solution)/shard_map/reduce_scatter | solution.py:233
  602.1 50.9 %reduce-scatter.16.cloned.1.call-done = f32[272,1088]{1,0:T(8,128)} async-done(((f32[1088,1088]{1,0:T(8,128)}), f32[272,1088]{1,0:T(8,128)}) %reduce-scatter.16.cloned.1.call-update) | async-done | bytes 1183760
  653.0 175.5 %reduce-scatter.12.cloned.1.call-done = f32[272,4352]{1,0:T(8,128)} async-done(((f32[1088,4352]{1,0:T(8,128)}), f32[272,4352]{1,0:T(8,128)}) %reduce-scatter.12.cloned.1.call-update) | async-done | bytes 4734992 | tf_op jit(solution)/shard_map/reduce_scatter | solution.py:249
  828.5 183.5 %reduce-scatter.14.cloned.1.call-done = f32[1088,1088]{1,0:T(8,128)} async-done(((f32[4352,1088]{1,0:T(8,128)}), f32[1088,1088]{1,0:T(8,128)}) %reduce-scatter.14.cloned.1.call-update) | async-done | bytes 4734992 | tf_op jit(solution)/shard_map/reduce_scatter | solution.py:252
  1012.0 139.2 %reduce-scatter.10.cloned.1.call-done = f32[272,3264]{1,0:T(8,128)} async-done(((f32[1088,3264]{1,0:T(8,128)}), f32[272,3264]{1,0:T(8,128)}) %reduce-scatter.10.cloned.1.call-update) | async-done | bytes 3551248 | tf_op jit(solution)/shard_map/reduce_scatter | solution.py:243
  1152.2 8.1 fusion.3
  1161.3 69.7 %all-gather.24.cloned.1.call-done = bf16[1088,3264]{1,0:T(8,128)(2,1)} async-done(((bf16[272,3264]{1,0:T(8,128)(2,1)}), bf16[1088,3264]{1,0:T(8,128)(2,1)}) %all-gather.24.cloned.1.call-update) | async-done | bytes 7102480 | tf_op jit(solution)/shard_map/all_gather | solution.py:147
  1237.7 43.1 %all-reduce.1 = (f32[1088]{0:T(1024)}, f32[1088]{0:T(1024)}, f32[2,1088]{1,0:T(2,128)}, f32[1088]{0:T(1024)}, f32[1088]{0:T(1024)}, /*index=5*/f32[1088]{0:T(1024)}, f32[4352]{0:T(1024)}, f32[1088]{0:T(1024)}) all-reduce(f32[1088]{0:T(1024)S(1)} %get-tuple-element.69, ...), channel_id=1, replica_groups=mesh['fsdp'=4,'ctx'=8] {'fsdp','ctx'}, use_global_device_ids=true, to_apply=%region_13.14 | all-reduce | flops 13056 | bytes 104448 | tf_op jit(solution)/shard_map/psum | solution.py:258
  1280.8 247.7 %all-reduce.5.cloned.1.call-done = (f32[272,3264]{1,0:T(8,128)}, f32[272,1088]{1,0:T(8,128)}, f32[272,4352]{1,0:T(8,128)}, f32[1088,1088]{1,0:T(8,128)}) async-done(((f32[272,3264]{1,0:T(8,128)}, f32[272,1088]{1,0:T(8,128)}, f32[272,4352]{1,0:T(8,128)}, f32[1088,1088]{1,0:T(8,128)}), (f32[272,3264]{1,0:T(8,128)}, f32[272,1088]{1,0:T(8,128)}, f32[272,4352]{1,0:T(8,128)}, ...) | async-done | bytes 14204944 | tf_op jit(solution)/shard_map/psum | solution.py:255
  (216 shorter events, 133.4 us)
Async XLA Ops:
  7.2 163.9 %all-gather.12.cloned.1.call-start = ((), (), s32[]{:S(2)}) async-start(), calls=%async_computation.6 | async-start | bytes 2654208 | tf_op jit(solution)/shard_map/all_gather | solution.py:123
  7.2 43.7 %collective-permute-start = (bf16[272,3264]{1,0:T(8,128)(2,1)}, bf16[272,3264]{1,0:T(8,128)(2,1)S(1)}, u32[]{:S(2)}, u32[]{:S(2)}) collective-permute-start(bf16[272,3264]{1,0:T(8,128)(2,1)} %param.21), channel_id=1, source_target_pairs={{0,8},{8,16},{16,24},{24,0},{1,9},{9,17},{17,25},{25,1},{2,10},{10... | collective-permute-start | bytes 5326856 | tf_op jit(solution)/shard_map/ppermute | solution.py:16
  50.9 41.7 %collective-permute-start.1 = (bf16[272,3264]{1,0:T(8,128)(2,1)S(1)}, bf16[272,3264]{1,0:T(8,128)(2,1)}, u32[]{:S(2)}, u32[]{:S(2)}) collective-permute-start(bf16[272,3264]{1,0:T(8,128)(2,1)S(1)} %collective-permute-done), channel_id=1, source_target_pairs={{0,8},{8,16},{16,24},{24,0},{1,9},{9,17},{17,25},{25,1},{2,10},{10... | collective-permute-start | bytes 5326856 | tf_op jit(solution)/shard_map/ppermute | solution.py:16
  92.6 41.0 %collective-permute-start.2 = (bf16[272,3264]{1,0:T(8,128)(2,1)}, bf16[272,3264]{1,0:T(8,128)(2,1)}, u32[]{:S(2)}, u32[]{:S(2)}) collective-permute-start(bf16[272,3264]{1,0:T(8,128)(2,1)} %collective-permute-done.1), channel_id=1, source_target_pairs={{0,8},{8,16},{16,24},{24,0},{1,9},{9,17},{17,25},{25,1},{2,10},{10... | collective-permute-start | bytes 5326856 | tf_op jit(solution)/shard_map/ppermute | solution.py:16
  139.5 64.4 %all-gather.10.cloned.1.call-start = ((), (), s32[]{:S(2)}) async-start(), calls=%async_computation.5 | async-start | bytes 2654208 | tf_op jit(solution)/shard_map/all_gather | solution.py:124
  140.9 102.8 %all-gather.14.cloned.1.call-start = ((), (), s32[]{:S(2)}) async-start(), calls=%async_computation.7 | async-start | bytes 3133440 | tf_op jit(solution)/shard_map/all_gather | solution.py:69
  141.7 204.8 %all-gather.18.cloned.1.call-start = ((), (), s32[]{:S(2)}) async-start(), calls=%async_computation.9 | async-start | bytes 12533760 | tf_op jit(solution)/shard_map/all_gather | solution.py:71
  142.3 302.4 %all-gather.16.cloned.1.call-start = ((), (), s32[]{:S(2)}) async-start(), calls=%async_computation.8 | async-start | bytes 11837440 | tf_op jit(solution)/shard_map/all_gather | solution.py:70
  142.9 339.4 %all-gather.20.cloned.1.call-start = ((), (), s32[]{:S(2)}) async-start(), calls=%async_computation.10 | async-start | bytes 2654208 | tf_op jit(solution)/shard_map/all_gather | solution.py:170
  157.1 362.5 %all-gather.22.cloned.1.call-start = ((), (), s32[]{:S(2)}) async-start(), calls=%async_computation.11 | async-start | bytes 2654208 | tf_op jit(solution)/shard_map/all_gather | solution.py:171
  211.2 247.6 %copy-start.9 = (bf16[128,1088]{0,1:T(8,128)(2,1)}, bf16[128,1088]{0,1:T(8,128)(2,1)S(1)}, u32[]{:S(2)}) copy-start(bf16[128,1088]{0,1:T(8,128)(2,1)S(1)} %reshape.201) | copy-start | bytes 835588
  211.3 135.3 %copy-start.13 = (bf16[2,64,1088]{2,1,0:T(8,128)(2,1)S(1)}, bf16[2,64,1088]{2,1,0:T(8,128)(2,1)}, u32[]{:S(2)}) copy-start(bf16[2,64,1088]{2,1,0:T(8,128)(2,1)} %param.31) | copy-start | bytes 835588
  246.6 211.3 %copy-start.33 = (f32[128]{0:T(128)}, f32[128]{0:T(128)S(1)}, u32[]{:S(2)}) copy-start(f32[128]{0:T(128)S(1)} %broadcast_multiply_fusion.6) | copy-start | bytes 1540
  246.7 211.1 %copy-start.39 = (f32[128]{0:T(128)}, f32[128]{0:T(128)S(1)}, u32[]{:S(2)}) copy-start(f32[128]{0:T(128)S(1)} %add_rsqrt_fusion.1) | copy-start | bytes 1540
  246.8 198.0 %copy-start.23 = (f32[1088]{0:T(1024)S(1)}, f32[1088]{0:T(1024)}, u32[]{:S(2)}) copy-start(f32[1088]{0:T(1024)} %param.25) | copy-start | bytes 13060
  246.8 198.0 %copy-start.25 = (f32[1088]{0:T(1024)S(1)}, f32[1088]{0:T(1024)}, u32[]{:S(2)}) copy-start(f32[1088]{0:T(1024)} %param.26) | copy-start | bytes 13060
  246.8 198.0 %copy-start.44 = (f32[4352]{0:T(1024)S(1)}, f32[4352]{0:T(1024)}, u32[]{:S(2)}) copy-start(f32[4352]{0:T(1024)} %param.28) | copy-start | bytes 52228
  461.4 130.0 %reduce-scatter.8.cloned.1.call-start = ((), (), s32[]{:S(2)}) async-start(), calls=%async_computation.12 | async-start | bytes 5308416 | tf_op jit(solution)/shard_map/reduce_scatter | solution.py:233
  537.1 115.8 %reduce-scatter.16.cloned.1.call-start = ((), (), s32[]{:S(2)}) async-start(), calls=%async_computation.17 | async-start | bytes 6266880
  541.5 287.1 %reduce-scatter.12.cloned.1.call-start = ((), (), s32[]{:S(2)}) async-start(), calls=%async_computation.15 | async-start | bytes 23674880 | tf_op jit(solution)/shard_map/reduce_scatter | solution.py:249
  551.7 460.3 %reduce-scatter.14.cloned.1.call-start = ((), (), s32[]{:S(2)}) async-start(), calls=%async_computation.16 | async-start | bytes 25067520 | tf_op jit(solution)/shard_map/reduce_scatter | solution.py:252
  563.6 587.6 %reduce-scatter.10.cloned.1.call-start = ((), (), s32[]{:S(2)}) async-start(), calls=%async_computation.14 | async-start | bytes 18104320 | tf_op jit(solution)/shard_map/reduce_scatter | solution.py:243
  601.1 629.9 %all-gather.24.cloned.1.call-start = ((), (), s32[]{:S(2)}) async-start(), calls=%async_computation.13 | async-start | bytes 9052160 | tf_op jit(solution)/shard_map/all_gather | solution.py:147
  601.8 926.6 %all-reduce.5.cloned.1.call-start = ((), (), s32[]{:S(2)}) async-start(), calls=%async_computation.18 | async-start | bytes 29245440 | tf_op jit(solution)/shard_map/psum | solution.py:255
  (42 other events, 454.2 us)
Sparse Core Ops, SparseCore 0:
  139.7 31.3 all-gather.11
  173.3 30.6 all-gather.9
  205.8 37.8 all-gather.13
  245.4 101.0 all-gather.17
  348.2 96.4 all-gather.15
  446.8 35.3 all-gather.19
  484.3 35.1 all-gather.21
  537.2 54.1 reduce-scatter.7
  595.1 57.8 reduce-scatter.15
  655.9 172.5 reduce-scatter.11
  831.7 180.2 reduce-scatter.13
  1015.0 136.1 reduce-scatter.9
  1153.1 77.9 all-gather.23
  1233.5 294.8 all-reduce.4
